TPU v7x, 256 devices: a whole 4x4x8 slice. The times are simulated.
256 devices in a mesh: clu: 32 (over x, y, core), sub: 8 (over z).
Axes of the slice: x: 4, y: 4, z: 8, core: 2. Of those that a mesh axis runs over, the one named last changes fastest.
Arguments:
- load_cases: float32 [128, 393216], P(None, ('clu', 'sub')), may hold values from -90 to 90
- initial: float32 [128, 393216], P(None, ('clu', 'sub')), may hold values from -6 to 6
- dual_blocks: bfloat16 [393216, 1536], P(('clu', 'sub')), may hold values from -1 to 3, as said below
- dirichlet: bfloat16 [393216, 1536], P(('clu', 'sub')), may hold values from -1 to 3, as said below
- rigid_modes: float32 [16384, 1536], P(('clu', 'sub')), may hold values from -1 to 1
- coarse_inverse: float32 [16384, 512], P(('clu', 'sub')), may hold values from -2 to 2, as said below
- face_block: int32 [256, 12], P(('clu', 'sub')), may hold values from 0 to 11, each once within a row
- active: int32 [256, 4], P(('clu', 'sub')), may hold values from 0 to 1, as said below
- membership: int32 [256], P('clu'), may hold values from 0 to 1
Outputs:
- multipliers: float32 [128, 393216], P(None, ('clu', 'sub'))
- residual: float32 [128, 393216], P(None, ('clu', 'sub'))
Inputs may be any that keep to these rules, and one draw needn't show every extreme that they name: active[s, g] equals active[p, g] for the partner p of subdomain s in colour g. `coarse_inverse`: each cluster's 512 rows form the inverse of the symmetric positive definite matrix C C^T + 0.5 I, where C stacks the rigid_modes rows of the cluster's subdomains. `dual_blocks`: each subdomain's block is symmetric. `dirichlet`: each subdomain's block is symmetric.
All inputs are finite; a program needn't handle non-finite values.
Results may differ from a plain program's by a relative error of at most 0.0022.
Values sent between devices are 32-bit elements; how exact they have to be, the bound alone decides.
No kernel may reach another device: no remote copies, remote signals or barrier semaphores. Data moves between devices by JAX's collectives and lax.ppermute only.
A program may use at most 64 MiB of HBM per device.

v0:
```python
import jax
import jax.numpy as jnp
from jax import lax
from jax.sharding import PartitionSpec as P

BLK = 128
E = 64
NCOL = 4
ITERS = 3
HIGH = lax.Precision.HIGHEST


def from_partner(value, axis, bit):
    mask = 2**bit
    pairs = [(source, source ^ mask) for source in range(lax.axis_size(axis))]
    return lax.ppermute(value, axis, pairs)


def on_device(
    load_cases,
    initial,
    dual_blocks,
    dirichlet,
    rigid_modes,
    coarse_inverse,
    face_block,
    active,
    membership,
):
    cases = load_cases.shape[0]
    blocks = dual_blocks.shape[0] // BLK
    per_colour = blocks // NCOL
    onehot = (face_block[0][:, None] == jnp.arange(blocks)[None, :]).astype(jnp.float32)
    edge_gates = active[0].astype(jnp.float32)
    own_index = lax.axis_index("sub")
    my_group = lax.dynamic_slice_in_dim(membership, own_index, 1)[0]
    same_group = (membership == my_group).astype(jnp.float32)

    def apply_local(vector, matrix):
        return jnp.dot(vector.astype(jnp.bfloat16), matrix, preferred_element_type=jnp.float32)

    def assemble(product):
        blocked = product.reshape(cases, blocks, BLK)
        slot_vals = jnp.einsum("jq,kqb->kjb", onehot, blocked, precision=HIGH)
        received = []
        for colour in range(NCOL - 1):
            outgoing = slot_vals[:, colour * per_colour : (colour + 1) * per_colour, :]
            incoming = from_partner(outgoing, "clu", colour)
            received.append(incoming * edge_gates[colour])
        outgoing_last = slot_vals[:, (NCOL - 1) * per_colour :, :]
        incoming_last = from_partner(outgoing_last, "sub", 0)
        received.append(incoming_last * edge_gates[NCOL - 1])
        joined = jnp.concatenate(received, axis=1)
        added = jnp.einsum("jq,kjb->kqb", onehot, joined, precision=HIGH)
        return product + added.reshape(cases, blocks * BLK)

    def coarse(vector):
        coeffs = jnp.einsum("em,km->ek", rigid_modes, vector, precision=HIGH)
        flat = coeffs.reshape(1, E * cases)
        piece = lax.all_gather(flat, "sub", axis=0, tiled=True)
        count = piece.shape[0]
        masked = (piece.reshape(count, E, cases) * same_group[:, None, None]).reshape(
            count * E, cases
        )
        amounts = jnp.dot(coarse_inverse, masked, precision=HIGH)
        correction = jnp.einsum("ek,em->km", amounts, rigid_modes, precision=HIGH)
        return vector - correction

    residual = coarse(load_cases - assemble(apply_local(initial, dual_blocks)))
    multipliers = initial
    for step in range(ITERS):
        search = coarse(assemble(apply_local(residual, dirichlet)))
        image = coarse(assemble(apply_local(search, dual_blocks)))
        cross_sum = jnp.sum(residual * image, axis=1)
        image_sum = jnp.sum(image * image, axis=1)
        cross_all, image_all = lax.psum((cross_sum, image_sum), ("clu", "sub"))
        step_len = cross_all / (image_all + 1e-06)
        multipliers = multipliers + step_len[:, None] * search
        residual = residual - step_len[:, None] * image
    return (multipliers, residual)


def solution(mesh):
    in_specs = (
        P(None, ("clu", "sub")),
        P(None, ("clu", "sub")),
        P(("clu", "sub"), None),
        P(("clu", "sub"), None),
        P(("clu", "sub"), None),
        P(("clu", "sub"), None),
        P(("clu", "sub"), None),
        P(("clu", "sub"), None),
        P("clu"),
    )
    out_specs = (P(None, ("clu", "sub")), P(None, ("clu", "sub")))
    return jax.shard_map(
        on_device, mesh=mesh, in_specs=in_specs, out_specs=out_specs, check_vma=False
    )
```

profile of v0, /device:TPU:1, one launch (start us, length us, event | category | flops | bytes accessed | tf_op | source)
XLA Modules:
  0.0 650.1 jit_solution(13790412827187783038)
XLA Ops:
  0.7 3.4 fusion.61
  5.7 3.3 collective-permute-start
  9.0 2.8 collective-permute-start.2
  18.8 5.1 collective-permute-done.1
  30.4 22.0 %all-gather = f32[8,1,8192]{2,1,0:T(1,128)S(1)} all-gather(f32[1,1,8192]{2,1,0:T(1,128)S(1)} %bitcast.168), channel_id=1, replica_groups=mesh['clu'=32,'sub'=8] {'sub'}, dimensions={0}, use_global_device_ids=true | all-gather | bytes 294912 | tf_op jit(solution)/shard_map/all_gather | solution.py:60
  54.8 3.1 fusion.59
  61.6 7.0 %collective-permute-start.4 = (f32[128,3,128]{2,1,0:T(4,128)S(1)}, f32[128,3,128]{2,1,0:T(4,128)S(1)}, u32[]{:S(2)}, u32[]{:S(2)}) collective-permute-start(f32[128,3,128]{2,1,0:T(4,128)S(1)} %get-tuple-element.34), channel_id=1, source_target_pairs={{0,8},{8,0},{16,24},{24,16},{32,40},{40,32},{48,56},{56,48},{64,72... | collective-permute-start | bytes 589832 | tf_op jit(solution)/shard_map/ppermute | solution.py:16
  71.9 4.5 collective-permute-done.7
  79.0 3.3 collective-permute-done.5
  90.0 19.1 %all-gather.1 = f32[8,1,8192]{2,1,0:T(1,128)S(1)} all-gather(f32[1,1,8192]{2,1,0:T(1,128)S(1)} %bitcast.169), channel_id=1, replica_groups=mesh['clu'=32,'sub'=8] {'sub'}, dimensions={0}, use_global_device_ids=true | all-gather | bytes 294912 | tf_op jit(solution)/shard_map/all_gather | solution.py:60
  110.3 3.1 fusion.57
  114.6 2.5 copy.64
  119.2 6.9 %collective-permute-start.8 = (f32[128,3,128]{2,1,0:T(4,128)S(1)}, f32[128,3,128]{2,1,0:T(4,128)S(1)}, u32[]{:S(2)}, u32[]{:S(2)}) collective-permute-start(f32[128,3,128]{2,1,0:T(4,128)S(1)} %get-tuple-element.30), channel_id=1, source_target_pairs={{0,8},{8,0},{16,24},{24,16},{32,40},{40,32},{48,56},{56,48},{64,72... | collective-permute-start | bytes 589832 | tf_op jit(solution)/shard_map/ppermute | solution.py:16
  126.1 3.5 collective-permute-start.10
  130.3 3.5 collective-permute-done.11
  136.5 3.9 collective-permute-done.9
  143.2 2.4 copy.66
  150.1 18.5 %all-gather.2 = f32[8,1,8192]{2,1,0:T(1,128)S(1)} all-gather(f32[1,1,8192]{2,1,0:T(1,128)S(1)} %bitcast.170), channel_id=1, replica_groups=mesh['clu'=32,'sub'=8] {'sub'}, dimensions={0}, use_global_device_ids=true | all-gather | bytes 294912 | tf_op jit(solution)/shard_map/all_gather | solution.py:60
  170.8 81.3 %all-reduce.2 = (f32[128]{0:T(128)S(1)}, f32[128]{0:T(128)S(1)}) all-reduce(f32[128]{0:T(128)S(1)} %get-tuple-element.7, f32[128]{0:T(128)S(1)} %get-tuple-element.6), channel_id=1, replica_groups=mesh['clu'=32,'sub'=8] {'clu','sub'}, use_global_device_ids=true, to_apply=%region_1.0 | all-reduce | flops 256 | bytes 2048 | tf_op jit(solution)/shard_map/psum | solution.py:76
  253.4 3.1 fusion.55
  257.6 2.5 copy.69
  267.4 3.4 collective-permute-done.15
  273.9 4.4 collective-permute-done.13
  281.1 2.4 copy.71
  287.9 19.2 %all-gather.3 = f32[8,1,8192]{2,1,0:T(1,128)S(1)} all-gather(f32[1,1,8192]{2,1,0:T(1,128)S(1)} %bitcast.171), channel_id=1, replica_groups=mesh['clu'=32,'sub'=8] {'sub'}, dimensions={0}, use_global_device_ids=true | all-gather | bytes 294912 | tf_op jit(solution)/shard_map/all_gather | solution.py:60
  308.3 3.1 fusion.53
  312.6 2.5 copy.74
  317.1 7.0 %collective-permute-start.16 = (f32[128,3,128]{2,1,0:T(4,128)S(1)}, f32[128,3,128]{2,1,0:T(4,128)S(1)}, u32[]{:S(2)}, u32[]{:S(2)}) collective-permute-start(f32[128,3,128]{2,1,0:T(4,128)S(1)} %get-tuple-element.22), channel_id=1, source_target_pairs={{0,8},{8,0},{16,24},{24,16},{32,40},{40,32},{48,56},{56,48},{64,72... | collective-permute-start | bytes 589832 | tf_op jit(solution)/shard_map/ppermute | solution.py:16
  327.0 4.9 collective-permute-done.19
  334.0 3.4 collective-permute-done.17
  340.2 2.4 copy.76
  347.0 18.4 %all-gather.4 = f32[8,1,8192]{2,1,0:T(1,128)S(1)} all-gather(f32[1,1,8192]{2,1,0:T(1,128)S(1)} %bitcast.172), channel_id=1, replica_groups=mesh['clu'=32,'sub'=8] {'sub'}, dimensions={0}, use_global_device_ids=true | all-gather | bytes 294912 | tf_op jit(solution)/shard_map/all_gather | solution.py:60
  368.5 80.5 %all-reduce.1 = (f32[128]{0:T(128)S(1)}, f32[128]{0:T(128)S(1)}) all-reduce(f32[128]{0:T(128)S(1)} %get-tuple-element.5, f32[128]{0:T(128)S(1)} %get-tuple-element.4), channel_id=1, replica_groups=mesh['clu'=32,'sub'=8] {'clu','sub'}, use_global_device_ids=true, to_apply=%region_5.0 | all-reduce | flops 256 | bytes 2048 | tf_op jit(solution)/shard_map/psum | solution.py:76
  450.3 3.1 fusion.51
  454.6 2.5 copy.79
  463.0 4.9 collective-permute-done.23
  471.0 2.7 collective-permute-done.21
  476.6 2.4 copy.81
  483.4 19.4 %all-gather.5 = f32[8,1,8192]{2,1,0:T(1,128)S(1)} all-gather(f32[1,1,8192]{2,1,0:T(1,128)S(1)} %bitcast.173), channel_id=1, replica_groups=mesh['clu'=32,'sub'=8] {'sub'}, dimensions={0}, use_global_device_ids=true | all-gather | bytes 294912 | tf_op jit(solution)/shard_map/all_gather | solution.py:60
  505.8 3.1 fusion.49
  510.1 2.5 copy.84
  514.7 7.0 %collective-permute-start.24 = (f32[128,3,128]{2,1,0:T(4,128)S(1)}, f32[128,3,128]{2,1,0:T(4,128)S(1)}, u32[]{:S(2)}, u32[]{:S(2)}) collective-permute-start(f32[128,3,128]{2,1,0:T(4,128)S(1)} %get-tuple-element.14), channel_id=1, source_target_pairs={{0,8},{8,0},{16,24},{24,16},{32,40},{40,32},{48,56},{56,48},{64,72... | collective-permute-start | bytes 589832 | tf_op jit(solution)/shard_map/ppermute | solution.py:16
  525.5 4.0 collective-permute-done.27
  531.5 5.0 collective-permute-done.25
  539.4 2.4 copy.86
  546.2 18.4 %all-gather.6 = f32[8,1,8192]{2,1,0:T(1,128)S(1)} all-gather(f32[1,1,8192]{2,1,0:T(1,128)S(1)} %bitcast.174), channel_id=1, replica_groups=mesh['clu'=32,'sub'=8] {'sub'}, dimensions={0}, use_global_device_ids=true | all-gather | bytes 294912 | tf_op jit(solution)/shard_map/all_gather | solution.py:60
  567.7 78.6 %all-reduce = (f32[128]{0:T(128)}, f32[128]{0:T(128)}) all-reduce(f32[128]{0:T(128)S(1)} %get-tuple-element.3, f32[128]{0:T(128)S(1)} %get-tuple-element.2), channel_id=1, replica_groups=mesh['clu'=32,'sub'=8] {'clu','sub'}, use_global_device_ids=true, to_apply=%region_9.0 | all-reduce | flops 256 | bytes 2048 | tf_op jit(solution)/shard_map/psum | solution.py:76
  647.0 2.9 multiply_subtract_fusion
  (155 shorter events, 133.0 us)
Async XLA Ops:
  0.6 27.7 %copy-start = (f32[64,1536]{1,0:T(8,128)S(1)}, f32[64,1536]{1,0:T(8,128)}, u32[]{:S(2)}) copy-start(f32[64,1536]{1,0:T(8,128)} %param.13) | copy-start | bytes 1179652
  0.6 4.2 copy-start.4
  4.1 8.2 %copy-start.5 = (s32[8]{0:T(128)S(1)}, s32[8]{0:T(128)}, u32[]{:S(2)}) copy-start(s32[8]{0:T(128)} %param.17) | copy-start | bytes 100
  4.1 9.4 %copy-start.6 = (s32[1,4]{1,0:T(1,128)S(1)}, s32[1,4]{1,0:T(1,128)}, u32[]{:S(2)}) copy-start(s32[1,4]{1,0:T(1,128)} %param.16) | copy-start | bytes 52
  5.7 8.6 %collective-permute-start = (f32[128,3,128]{2,1,0:T(4,128)S(1)}, f32[128,3,128]{2,1,0:T(4,128)S(1)}, u32[]{:S(2)}, u32[]{:S(2)}) collective-permute-start(f32[128,3,128]{2,1,0:T(4,128)S(1)} %get-tuple-element.38), channel_id=1, source_target_pairs={{0,8},{8,0},{16,24},{24,16},{32,40},{40,32},{48,56},{56,48},{64,72... | collective-permute-start | bytes 589832 | tf_op jit(solution)/shard_map/ppermute | solution.py:16
  9.0 7.8 %collective-permute-start.3 = (f32[128,3,128]{2,1,0:T(4,128)S(1)}, f32[128,3,128]{2,1,0:T(4,128)S(1)}, u32[]{:S(2)}, u32[]{:S(2)}) collective-permute-start(f32[128,3,128]{2,1,0:T(4,128)S(1)} %get-tuple-element.39), channel_id=1, source_target_pairs={{0,1},{1,0},{2,3},{3,2},{4,5},{5,4},{6,7},{7,6},{8,9},{9,8},{10,11... | collective-permute-start | bytes 589832 | tf_op jit(solution)/shard_map/ppermute | solution.py:16
  9.0 9.1 %collective-permute-start.2 = (f32[128,3,128]{2,1,0:T(4,128)S(1)}, f32[128,3,128]{2,1,0:T(4,128)S(1)}, u32[]{:S(2)}, u32[]{:S(2)}) collective-permute-start(f32[128,3,128]{2,1,0:T(4,128)S(1)} %get-tuple-element.40), channel_id=1, source_target_pairs={{0,32},{8,40},{16,48},{24,56},{32,0},{40,8},{48,16},{56,24},{64,96... | collective-permute-start | bytes 589832 | tf_op jit(solution)/shard_map/ppermute | solution.py:16
  11.8 12.0 %collective-permute-start.1 = (f32[128,3,128]{2,1,0:T(4,128)S(1)}, f32[128,3,128]{2,1,0:T(4,128)S(1)}, u32[]{:S(2)}, u32[]{:S(2)}) collective-permute-start(f32[128,3,128]{2,1,0:T(4,128)S(1)} %get-tuple-element.41), channel_id=1, source_target_pairs={{0,16},{8,24},{16,0},{24,8},{32,48},{40,56},{48,32},{56,40},{64,80... | collective-permute-start | bytes 589832 | tf_op jit(solution)/shard_map/ppermute | solution.py:16
  18.1 34.3 %copy-start.3 = (f32[64,512]{1,0:T(8,128)S(1)}, f32[64,512]{1,0:T(8,128)}, u32[]{:S(2)}) copy-start(f32[64,512]{1,0:T(8,128)} %param.14) | copy-start | bytes 393220
  61.6 9.5 %collective-permute-start.4 = (f32[128,3,128]{2,1,0:T(4,128)S(1)}, f32[128,3,128]{2,1,0:T(4,128)S(1)}, u32[]{:S(2)}, u32[]{:S(2)}) collective-permute-start(f32[128,3,128]{2,1,0:T(4,128)S(1)} %get-tuple-element.34), channel_id=1, source_target_pairs={{0,8},{8,0},{16,24},{24,16},{32,40},{40,32},{48,56},{56,48},{64,72... | collective-permute-start | bytes 589832 | tf_op jit(solution)/shard_map/ppermute | solution.py:16
  68.6 7.8 %collective-permute-start.7 = (f32[128,3,128]{2,1,0:T(4,128)S(1)}, f32[128,3,128]{2,1,0:T(4,128)S(1)}, u32[]{:S(2)}, u32[]{:S(2)}) collective-permute-start(f32[128,3,128]{2,1,0:T(4,128)S(1)} %get-tuple-element.35), channel_id=1, source_target_pairs={{0,1},{1,0},{2,3},{3,2},{4,5},{5,4},{6,7},{7,6},{8,9},{9,8},{10,11... | collective-permute-start | bytes 589832 | tf_op jit(solution)/shard_map/ppermute | solution.py:16
  69.4 9.0 %collective-permute-start.6 = (f32[128,3,128]{2,1,0:T(4,128)S(1)}, f32[128,3,128]{2,1,0:T(4,128)S(1)}, u32[]{:S(2)}, u32[]{:S(2)}) collective-permute-start(f32[128,3,128]{2,1,0:T(4,128)S(1)} %get-tuple-element.36), channel_id=1, source_target_pairs={{0,32},{8,40},{16,48},{24,56},{32,0},{40,8},{48,16},{56,24},{64,96... | collective-permute-start | bytes 589832 | tf_op jit(solution)/shard_map/ppermute | solution.py:16
  71.0 11.4 %collective-permute-start.5 = (f32[128,3,128]{2,1,0:T(4,128)S(1)}, f32[128,3,128]{2,1,0:T(4,128)S(1)}, u32[]{:S(2)}, u32[]{:S(2)}) collective-permute-start(f32[128,3,128]{2,1,0:T(4,128)S(1)} %get-tuple-element.37), channel_id=1, source_target_pairs={{0,16},{8,24},{16,0},{24,8},{32,48},{40,56},{48,32},{56,40},{64,80... | collective-permute-start | bytes 589832 | tf_op jit(solution)/shard_map/ppermute | solution.py:16
  119.2 10.4 %collective-permute-start.8 = (f32[128,3,128]{2,1,0:T(4,128)S(1)}, f32[128,3,128]{2,1,0:T(4,128)S(1)}, u32[]{:S(2)}, u32[]{:S(2)}) collective-permute-start(f32[128,3,128]{2,1,0:T(4,128)S(1)} %get-tuple-element.30), channel_id=1, source_target_pairs={{0,8},{8,0},{16,24},{24,16},{32,40},{40,32},{48,56},{56,48},{64,72... | collective-permute-start | bytes 589832 | tf_op jit(solution)/shard_map/ppermute | solution.py:16
  126.1 7.8 %collective-permute-start.11 = (f32[128,3,128]{2,1,0:T(4,128)S(1)}, f32[128,3,128]{2,1,0:T(4,128)S(1)}, u32[]{:S(2)}, u32[]{:S(2)}) collective-permute-start(f32[128,3,128]{2,1,0:T(4,128)S(1)} %get-tuple-element.31), channel_id=1, source_target_pairs={{0,1},{1,0},{2,3},{3,2},{4,5},{5,4},{6,7},{7,6},{8,9},{9,8},{10,11... | collective-permute-start | bytes 589832 | tf_op jit(solution)/shard_map/ppermute | solution.py:16
  126.1 9.8 %collective-permute-start.10 = (f32[128,3,128]{2,1,0:T(4,128)S(1)}, f32[128,3,128]{2,1,0:T(4,128)S(1)}, u32[]{:S(2)}, u32[]{:S(2)}) collective-permute-start(f32[128,3,128]{2,1,0:T(4,128)S(1)} %get-tuple-element.32), channel_id=1, source_target_pairs={{0,32},{8,40},{16,48},{24,56},{32,0},{40,8},{48,16},{56,24},{64,96... | collective-permute-start | bytes 589832 | tf_op jit(solution)/shard_map/ppermute | solution.py:16
  129.5 10.9 %collective-permute-start.9 = (f32[128,3,128]{2,1,0:T(4,128)S(1)}, f32[128,3,128]{2,1,0:T(4,128)S(1)}, u32[]{:S(2)}, u32[]{:S(2)}) collective-permute-start(f32[128,3,128]{2,1,0:T(4,128)S(1)} %get-tuple-element.33), channel_id=1, source_target_pairs={{0,16},{8,24},{16,0},{24,8},{32,48},{40,56},{48,32},{56,40},{64,80... | collective-permute-start | bytes 589832 | tf_op jit(solution)/shard_map/ppermute | solution.py:16
  262.2 4.4 collective-permute-start.12
  263.0 7.8 %collective-permute-start.15 = (f32[128,3,128]{2,1,0:T(4,128)S(1)}, f32[128,3,128]{2,1,0:T(4,128)S(1)}, u32[]{:S(2)}, u32[]{:S(2)}) collective-permute-start(f32[128,3,128]{2,1,0:T(4,128)S(1)} %get-tuple-element.27), channel_id=1, source_target_pairs={{0,1},{1,0},{2,3},{3,2},{4,5},{5,4},{6,7},{7,6},{8,9},{9,8},{10,11... | collective-permute-start | bytes 589832 | tf_op jit(solution)/shard_map/ppermute | solution.py:16
  264.2 9.0 %collective-permute-start.14 = (f32[128,3,128]{2,1,0:T(4,128)S(1)}, f32[128,3,128]{2,1,0:T(4,128)S(1)}, u32[]{:S(2)}, u32[]{:S(2)}) collective-permute-start(f32[128,3,128]{2,1,0:T(4,128)S(1)} %get-tuple-element.28), channel_id=1, source_target_pairs={{0,32},{8,40},{16,48},{24,56},{32,0},{40,8},{48,16},{56,24},{64,96... | collective-permute-start | bytes 589832 | tf_op jit(solution)/shard_map/ppermute | solution.py:16
  265.3 12.9 %collective-permute-start.13 = (f32[128,3,128]{2,1,0:T(4,128)S(1)}, f32[128,3,128]{2,1,0:T(4,128)S(1)}, u32[]{:S(2)}, u32[]{:S(2)}) collective-permute-start(f32[128,3,128]{2,1,0:T(4,128)S(1)} %get-tuple-element.29), channel_id=1, source_target_pairs={{0,16},{8,24},{16,0},{24,8},{32,48},{40,56},{48,32},{56,40},{64,80... | collective-permute-start | bytes 589832 | tf_op jit(solution)/shard_map/ppermute | solution.py:16
  317.1 9.1 %collective-permute-start.16 = (f32[128,3,128]{2,1,0:T(4,128)S(1)}, f32[128,3,128]{2,1,0:T(4,128)S(1)}, u32[]{:S(2)}, u32[]{:S(2)}) collective-permute-start(f32[128,3,128]{2,1,0:T(4,128)S(1)} %get-tuple-element.22), channel_id=1, source_target_pairs={{0,8},{8,0},{16,24},{24,16},{32,40},{40,32},{48,56},{56,48},{64,72... | collective-permute-start | bytes 589832 | tf_op jit(solution)/shard_map/ppermute | solution.py:16
  324.1 7.8 %collective-permute-start.19 = (f32[128,3,128]{2,1,0:T(4,128)S(1)}, f32[128,3,128]{2,1,0:T(4,128)S(1)}, u32[]{:S(2)}, u32[]{:S(2)}) collective-permute-start(f32[128,3,128]{2,1,0:T(4,128)S(1)} %get-tuple-element.23), channel_id=1, source_target_pairs={{0,1},{1,0},{2,3},{3,2},{4,5},{5,4},{6,7},{7,6},{8,9},{9,8},{10,11... | collective-permute-start | bytes 589832 | tf_op jit(solution)/shard_map/ppermute | solution.py:16
  324.1 9.2 %collective-permute-start.18 = (f32[128,3,128]{2,1,0:T(4,128)S(1)}, f32[128,3,128]{2,1,0:T(4,128)S(1)}, u32[]{:S(2)}, u32[]{:S(2)}) collective-permute-start(f32[128,3,128]{2,1,0:T(4,128)S(1)} %get-tuple-element.24), channel_id=1, source_target_pairs={{0,32},{8,40},{16,48},{24,56},{32,0},{40,8},{48,16},{56,24},{64,96... | collective-permute-start | bytes 589832 | tf_op jit(solution)/shard_map/ppermute | solution.py:16
  325.9 11.6 %collective-permute-start.17 = (f32[128,3,128]{2,1,0:T(4,128)S(1)}, f32[128,3,128]{2,1,0:T(4,128)S(1)}, u32[]{:S(2)}, u32[]{:S(2)}) collective-permute-start(f32[128,3,128]{2,1,0:T(4,128)S(1)} %get-tuple-element.25), channel_id=1, source_target_pairs={{0,16},{8,24},{16,0},{24,8},{32,48},{40,56},{48,32},{56,40},{64,80... | collective-permute-start | bytes 589832 | tf_op jit(solution)/shard_map/ppermute | solution.py:16
  459.1 3.1 collective-permute-start.20
  460.1 7.8 %collective-permute-start.23 = (f32[128,3,128]{2,1,0:T(4,128)S(1)}, f32[128,3,128]{2,1,0:T(4,128)S(1)}, u32[]{:S(2)}, u32[]{:S(2)}) collective-permute-start(f32[128,3,128]{2,1,0:T(4,128)S(1)} %get-tuple-element.19), channel_id=1, source_target_pairs={{0,1},{1,0},{2,3},{3,2},{4,5},{5,4},{6,7},{7,6},{8,9},{9,8},{10,11... | collective-permute-start | bytes 589832 | tf_op jit(solution)/shard_map/ppermute | solution.py:16
  461.4 9.0 %collective-permute-start.22 = (f32[128,3,128]{2,1,0:T(4,128)S(1)}, f32[128,3,128]{2,1,0:T(4,128)S(1)}, u32[]{:S(2)}, u32[]{:S(2)}) collective-permute-start(f32[128,3,128]{2,1,0:T(4,128)S(1)} %get-tuple-element.20), channel_id=1, source_target_pairs={{0,32},{8,40},{16,48},{24,56},{32,0},{40,8},{48,16},{56,24},{64,96... | collective-permute-start | bytes 589832 | tf_op jit(solution)/shard_map/ppermute | solution.py:16
  462.3 11.5 %collective-permute-start.21 = (f32[128,3,128]{2,1,0:T(4,128)S(1)}, f32[128,3,128]{2,1,0:T(4,128)S(1)}, u32[]{:S(2)}, u32[]{:S(2)}) collective-permute-start(f32[128,3,128]{2,1,0:T(4,128)S(1)} %get-tuple-element.21), channel_id=1, source_target_pairs={{0,16},{8,24},{16,0},{24,8},{32,48},{40,56},{48,32},{56,40},{64,80... | collective-permute-start | bytes 589832 | tf_op jit(solution)/shard_map/ppermute | solution.py:16
  504.9 0.9 copy-start.1
  514.7 10.0 %collective-permute-start.24 = (f32[128,3,128]{2,1,0:T(4,128)S(1)}, f32[128,3,128]{2,1,0:T(4,128)S(1)}, u32[]{:S(2)}, u32[]{:S(2)}) collective-permute-start(f32[128,3,128]{2,1,0:T(4,128)S(1)} %get-tuple-element.14), channel_id=1, source_target_pairs={{0,8},{8,0},{16,24},{24,16},{32,40},{40,32},{48,56},{56,48},{64,72... | collective-permute-start | bytes 589832 | tf_op jit(solution)/shard_map/ppermute | solution.py:16
  521.7 7.8 %collective-permute-start.27 = (f32[128,3,128]{2,1,0:T(4,128)S(1)}, f32[128,3,128]{2,1,0:T(4,128)S(1)}, u32[]{:S(2)}, u32[]{:S(2)}) collective-permute-start(f32[128,3,128]{2,1,0:T(4,128)S(1)} %get-tuple-element.15), channel_id=1, source_target_pairs={{0,1},{1,0},{2,3},{3,2},{4,5},{5,4},{6,7},{7,6},{8,9},{9,8},{10,11... | collective-permute-start | bytes 589832 | tf_op jit(solution)/shard_map/ppermute | solution.py:16
  521.7 9.2 %collective-permute-start.26 = (f32[128,3,128]{2,1,0:T(4,128)S(1)}, f32[128,3,128]{2,1,0:T(4,128)S(1)}, u32[]{:S(2)}, u32[]{:S(2)}) collective-permute-start(f32[128,3,128]{2,1,0:T(4,128)S(1)} %get-tuple-element.16), channel_id=1, source_target_pairs={{0,32},{8,40},{16,48},{24,56},{32,0},{40,8},{48,16},{56,24},{64,96... | collective-permute-start | bytes 589832 | tf_op jit(solution)/shard_map/ppermute | solution.py:16
  523.4 13.2 %collective-permute-start.25 = (f32[128,3,128]{2,1,0:T(4,128)S(1)}, f32[128,3,128]{2,1,0:T(4,128)S(1)}, u32[]{:S(2)}, u32[]{:S(2)}) collective-permute-start(f32[128,3,128]{2,1,0:T(4,128)S(1)} %get-tuple-element.17), channel_id=1, source_target_pairs={{0,16},{8,24},{16,0},{24,8},{32,48},{40,56},{48,32},{56,40},{64,80... | collective-permute-start | bytes 589832 | tf_op jit(solution)/shard_map/ppermute | solution.py:16
  545.3 101.8 %copy-start.2 = (f32[128,1536]{1,0:T(8,128)S(1)}, f32[128,1536]{1,0:T(8,128)}, u32[]{:S(2)}) copy-start(f32[128,1536]{1,0:T(8,128)} %copy-done.1) | copy-start | bytes 2359300
where the time goes:
time: 661 us; the launch traced here: 650 us
  blocking collectives  375 us (57%)
  matrix products  70.3 us (11%)
  waiting for transfers between devices  63.1 us (10%)
  starting transfers between devices  53 us (8%)
  local copies, waits for them, and re-layouts  52.9 us (8%)
  other arithmetic  33.6 us (5%)
    psum x3, blocking collectives, on_device(): cross_all, image_all = lax.psum((cross_sum, image_sum), ('clu', 'sub'))  240 us
    all_gather x7, blocking collectives, coarse(): piece = lax.all_gather(flat, 'sub', axis=0, tiled=True)  135 us
    ppermute x28, waiting for transfers between devices, from_partner(): return lax.ppermute(value, axis, pairs)  63.1 us
    ppermute x28, starting transfers between devices, from_partner(): return lax.ppermute(value, axis, pairs)  53 us
    dot_general x7, matrix products, apply_local(): jnp.dot(vector.astype(jnp.bfloat16), matrix, preferred_element_type=jnp.f...  22.2 us
    mul x21, other arithmetic, assemble(): received.append(incoming * edge_gates[colour])  14.8 us
    transpose x7, local copies, waits for them, and re-layouts, assemble(): added = jnp.einsum('jq,kjb->kqb', onehot, joined, precision=HIGH)  14.7 us
    reshape x7, local copies, waits for them, and re-layouts, assemble(): blocked = product.reshape(cases, blocks, BLK)  14.5 us
  transfers between devices with their start and end apart: 28, of which 21 were waited for; matrix products, arithmetic and copies ran while one was open for 3% of the time, Pallas kernels for 0%

commit v1 on v0

--- a/solution.py
+++ b/solution.py
@@ -8,6 +8,13 @@
 NCOL = 4
 ITERS = 3
 HIGH = lax.Precision.HIGHEST
+
+
+def exchange_gather(block, axis, dim):
+    size = lax.axis_size(axis)
+    pieces = jnp.stack([block for _ in range(size)])
+    pieces = lax.all_to_all(pieces, axis, split_axis=0, concat_axis=0)
+    return jnp.concatenate(pieces, axis=dim)
 
 
 def from_partner(value, axis, bit):
@@ -57,7 +64,7 @@
     def coarse(vector):
         coeffs = jnp.einsum("em,km->ek", rigid_modes, vector, precision=HIGH)
         flat = coeffs.reshape(1, E * cases)
-        piece = lax.all_gather(flat, "sub", axis=0, tiled=True)
+        piece = exchange_gather(flat, "sub", 0)
         count = piece.shape[0]
         masked = (piece.reshape(count, E, cases) * same_group[:, None, None]).reshape(
             count * E, cases

time: 661 us -> 597 us (0.903)
  blocking collectives: 375 us -> 309 us
  waiting for transfers between devices: 63.1 us -> 73.4 us
  starting transfers between devices: 53 us -> 44.3 us
    all_gather x7 -> x0, blocking collectives: 135 us -> none  [coarse(): piece = lax.all_gather(flat, 'sub', axis=0, tiled=True)]
    all_to_all x0 -> x6, blocking collectives: none -> 75.9 us  [exchange_gather(): pieces = lax.all_to_all(pieces, axis, split_axis=0, concat_axis=0)]
    ppermute x28, starting transfers between devices: 53 us -> 37 us  [from_partner(): return lax.ppermute(value, axis, pairs)]
    all_to_all x0 -> x1, waiting for transfers between devices: none -> 8.79 us  [exchange_gather(): pieces = lax.all_to_all(pieces, axis, split_axis=0, concat_axis=0)]
    psum x3, blocking collectives: 240 us -> 233 us  [on_device(): cross_all, image_all = lax.psum((cross_sum, image_sum), ('clu', 'sub'))]
    all_to_all x0 -> x1, starting transfers between devices: none -> 7.29 us  [exchange_gather(): pieces = lax.all_to_all(pieces, axis, split_axis=0, concat_axis=0)]
  transfers between devices with their start and end apart: 28 -> 29, of which waited for: 21 -> 22; matrix products, arithmetic and copies ran while one was open for 3% -> 3% of each run, Pallas kernels for 0% -> 0%
where the time goes in v1:
time: 597 us; the launch traced here: 586 us
  blocking collectives  309 us (52%)
  waiting for transfers between devices  73.4 us (12%)
  matrix products  70.4 us (12%)
  local copies, waits for them, and re-layouts  54.6 us (9%)
  starting transfers between devices  44.3 us (7%)
  other arithmetic  33 us (6%)
    psum x3, blocking collectives, on_device(): cross_all, image_all = lax.psum((cross_sum, image_sum), ('clu', 'sub'))  233 us
    all_to_all x6, blocking collectives, exchange_gather(): pieces = lax.all_to_all(pieces, axis, split_axis=0, concat_axis=0)  75.9 us
    ppermute x28, waiting for transfers between devices, from_partner(): return lax.ppermute(value, axis, pairs)  64.6 us
    ppermute x28, starting transfers between devices, from_partner(): return lax.ppermute(value, axis, pairs)  37 us
    dot_general x7, matrix products, apply_local(): jnp.dot(vector.astype(jnp.bfloat16), matrix, preferred_element_type=jnp.f...  22.2 us
    transpose x7, local copies, waits for them, and re-layouts, assemble(): added = jnp.einsum('jq,kjb->kqb', onehot, joined, precision=HIGH)  14.7 us
    reshape x7, local copies, waits for them, and re-layouts, assemble(): blocked = product.reshape(cases, blocks, BLK)  14.6 us
    reshape x7, local copies, waits for them, and re-layouts, assemble(): return product + added.reshape(cases, blocks * BLK)  13.9 us
  transfers between devices with their start and end apart: 29, of which 22 were waited for; matrix products, arithmetic and copies ran while one was open for 3% of the time, Pallas kernels for 0%

profile of v1, /device:TPU:1, one launch (start us, length us, event | category | flops | bytes accessed | tf_op | source)
XLA Modules:
  0.0 586.2 jit_solution(4157610508370626822)
XLA Ops:
  0.7 3.4 fusion.61
  5.7 3.3 collective-permute-start
  9.0 2.8 collective-permute-start.2
  13.6 3.2 collective-permute-done.3
  18.8 5.1 collective-permute-done.1
  31.1 7.3 %all-to-all-start = ((f32[8,1,8192]{2,1,0:T(1,128)}), f32[8,1,8192]{2,1,0:T(1,128)S(1)}, u32[]{:S(2)}, u32[]{:S(2)}) async-start(f32[8,1,8192]{2,1,0:T(1,128)} %stack.21), calls=%async_computation | async-start | bytes 524288 | tf_op jit(solution)/shard_map/all_to_all | solution.py:16
  39.8 8.8 %all-to-all-done = f32[8,1,8192]{2,1,0:T(1,128)S(1)} async-done(((f32[8,1,8192]{2,1,0:T(1,128)}), f32[8,1,8192]{2,1,0:T(1,128)S(1)}, u32[]{:S(2)}, u32[]{:S(2)}) %all-to-all-start) | async-done | bytes 262176 | tf_op jit(solution)/shard_map/all_to_all | solution.py:16
  51.1 3.1 fusion.59
  57.9 2.7 collective-permute-start.4
  63.4 5.0 collective-permute-done.7
  70.6 3.3 collective-permute-done.5
  81.6 12.7 %all_to_all.35 = f32[8,1,8192]{2,1,0:T(1,128)S(1)} all-to-all(f32[8,1,8192]{2,1,0:T(1,128)S(1)} %stack.22), channel_id=1, replica_groups=mesh['clu'=32,'sub'=8] {'sub'}, dimensions={0} | all-to-all | bytes 524288 | tf_op jit(solution)/shard_map/all_to_all | solution.py:16
  95.5 3.1 fusion.57
  99.8 2.5 copy.99
  104.3 2.6 collective-permute-start.8
  107.2 3.3 collective-permute-start.10
  111.2 3.5 collective-permute-done.11
  117.6 3.9 collective-permute-done.9
  124.1 2.4 copy.101
  131.1 12.6 %all_to_all.36 = f32[8,1,8192]{2,1,0:T(1,128)S(1)} all-to-all(f32[8,1,8192]{2,1,0:T(1,128)S(1)} %stack.23), channel_id=1, replica_groups=mesh['clu'=32,'sub'=8] {'sub'}, dimensions={0} | all-to-all | bytes 524288 | tf_op jit(solution)/shard_map/all_to_all | solution.py:16
  145.8 84.5 %all-reduce.2 = (f32[128]{0:T(128)S(1)}, f32[128]{0:T(128)S(1)}) all-reduce(f32[128]{0:T(128)S(1)} %get-tuple-element.7, f32[128]{0:T(128)S(1)} %get-tuple-element.6), channel_id=1, replica_groups=mesh['clu'=32,'sub'=8] {'clu','sub'}, use_global_device_ids=true, to_apply=%region_1.0 | all-reduce | flops 256 | bytes 2048 | tf_op jit(solution)/shard_map/psum | solution.py:83
  231.6 3.1 fusion.55
  235.8 2.5 copy.104
  246.1 3.4 collective-permute-done.15
  252.7 4.4 collective-permute-done.13
  259.8 2.4 copy.106
  266.7 12.6 %all_to_all.37 = f32[8,1,8192]{2,1,0:T(1,128)S(1)} all-to-all(f32[8,1,8192]{2,1,0:T(1,128)S(1)} %stack.24), channel_id=1, replica_groups=mesh['clu'=32,'sub'=8] {'sub'}, dimensions={0} | all-to-all | bytes 524288 | tf_op jit(solution)/shard_map/all_to_all | solution.py:16
  280.5 3.1 fusion.53
  284.8 2.5 copy.109
  289.4 2.8 collective-permute-start.16
  295.0 4.9 collective-permute-done.19
  302.3 3.6 collective-permute-done.17
  308.6 2.4 copy.111
  315.6 12.6 %all_to_all.38 = f32[8,1,8192]{2,1,0:T(1,128)S(1)} all-to-all(f32[8,1,8192]{2,1,0:T(1,128)S(1)} %stack.25), channel_id=1, replica_groups=mesh['clu'=32,'sub'=8] {'sub'}, dimensions={0} | all-to-all | bytes 524288 | tf_op jit(solution)/shard_map/all_to_all | solution.py:16
  331.2 75.0 %all-reduce.1 = (f32[128]{0:T(128)S(1)}, f32[128]{0:T(128)S(1)}) all-reduce(f32[128]{0:T(128)S(1)} %get-tuple-element.5, f32[128]{0:T(128)S(1)} %get-tuple-element.4), channel_id=1, replica_groups=mesh['clu'=32,'sub'=8] {'clu','sub'}, use_global_device_ids=true, to_apply=%region_5.0 | all-reduce | flops 256 | bytes 2048 | tf_op jit(solution)/shard_map/psum | solution.py:83
  407.5 3.1 fusion.51
  411.7 2.5 copy.114
  420.7 4.9 collective-permute-done.23
  428.7 2.9 collective-permute-done.21
  441.3 12.9 %all_to_all.39 = f32[8,1,8192]{2,1,0:T(1,128)S(1)} all-to-all(f32[8,1,8192]{2,1,0:T(1,128)S(1)} %stack.26), channel_id=1, replica_groups=mesh['clu'=32,'sub'=8] {'sub'}, dimensions={0} | all-to-all | bytes 524288 | tf_op jit(solution)/shard_map/all_to_all | solution.py:16
  457.2 3.1 fusion.49
  461.5 2.5 copy.119
  466.1 2.7 collective-permute-start.24
  472.6 4.0 collective-permute-done.27
  478.8 4.7 collective-permute-done.25
  493.2 12.6 %all_to_all.40 = f32[8,1,8192]{2,1,0:T(1,128)S(1)} all-to-all(f32[8,1,8192]{2,1,0:T(1,128)S(1)} %stack.27), channel_id=1, replica_groups=mesh['clu'=32,'sub'=8] {'sub'}, dimensions={0} | all-to-all | bytes 524288 | tf_op jit(solution)/shard_map/all_to_all | solution.py:16
  508.8 73.3 %all-reduce = (f32[128]{0:T(128)}, f32[128]{0:T(128)}) all-reduce(f32[128]{0:T(128)S(1)} %get-tuple-element.3, f32[128]{0:T(128)S(1)} %get-tuple-element.2), channel_id=1, replica_groups=mesh['clu'=32,'sub'=8] {'clu','sub'}, use_global_device_ids=true, to_apply=%region_9.0 | all-reduce | flops 256 | bytes 2048 | tf_op jit(solution)/shard_map/psum | solution.py:83
  582.9 2.9 multiply_subtract_fusion
  (163 shorter events, 137.9 us)
Async XLA Ops:
  0.6 27.6 %copy-start = (f32[64,1536]{1,0:T(8,128)S(1)}, f32[64,1536]{1,0:T(8,128)}, u32[]{:S(2)}) copy-start(f32[64,1536]{1,0:T(8,128)} %param.13) | copy-start | bytes 1179652
  0.6 4.2 copy-start.4
  4.1 8.1 %copy-start.5 = (s32[1,4]{1,0:T(1,128)S(1)}, s32[1,4]{1,0:T(1,128)}, u32[]{:S(2)}) copy-start(s32[1,4]{1,0:T(1,128)} %param.16) | copy-start | bytes 52
  5.7 7.2 %collective-permute-start = (f32[128,3,128]{2,1,0:T(4,128)S(1)}, f32[128,3,128]{2,1,0:T(4,128)S(1)}, u32[]{:S(2)}, u32[]{:S(2)}) collective-permute-start(f32[128,3,128]{2,1,0:T(4,128)S(1)} %get-tuple-element.38), channel_id=1, source_target_pairs={{0,8},{8,0},{16,24},{24,16},{32,40},{40,32},{48,56},{56,48},{64,72... | collective-permute-start | bytes 589832 | tf_op jit(solution)/shard_map/ppermute | solution.py:23
  9.0 7.8 %collective-permute-start.3 = (f32[128,3,128]{2,1,0:T(4,128)S(1)}, f32[128,3,128]{2,1,0:T(4,128)S(1)}, u32[]{:S(2)}, u32[]{:S(2)}) collective-permute-start(f32[128,3,128]{2,1,0:T(4,128)S(1)} %get-tuple-element.39), channel_id=1, source_target_pairs={{0,1},{1,0},{2,3},{3,2},{4,5},{5,4},{6,7},{7,6},{8,9},{9,8},{10,11... | collective-permute-start | bytes 589832 | tf_op jit(solution)/shard_map/ppermute | solution.py:23
  9.0 9.1 %collective-permute-start.2 = (f32[128,3,128]{2,1,0:T(4,128)S(1)}, f32[128,3,128]{2,1,0:T(4,128)S(1)}, u32[]{:S(2)}, u32[]{:S(2)}) collective-permute-start(f32[128,3,128]{2,1,0:T(4,128)S(1)} %get-tuple-element.40), channel_id=1, source_target_pairs={{0,32},{8,40},{16,48},{24,56},{32,0},{40,8},{48,16},{56,24},{64,96... | collective-permute-start | bytes 589832 | tf_op jit(solution)/shard_map/ppermute | solution.py:23
  11.8 12.0 %collective-permute-start.1 = (f32[128,3,128]{2,1,0:T(4,128)S(1)}, f32[128,3,128]{2,1,0:T(4,128)S(1)}, u32[]{:S(2)}, u32[]{:S(2)}) collective-permute-start(f32[128,3,128]{2,1,0:T(4,128)S(1)} %get-tuple-element.41), channel_id=1, source_target_pairs={{0,16},{8,24},{16,0},{24,8},{32,48},{40,56},{48,32},{56,40},{64,80... | collective-permute-start | bytes 589832 | tf_op jit(solution)/shard_map/ppermute | solution.py:23
  23.9 14.6 %copy-start.6 = (s32[8]{0:T(128)S(1)}, s32[8]{0:T(128)}, u32[]{:S(2)}) copy-start(s32[8]{0:T(128)} %param.17) | copy-start | bytes 100
  23.9 24.8 %copy-start.3 = (f32[64,512]{1,0:T(8,128)S(1)}, f32[64,512]{1,0:T(8,128)}, u32[]{:S(2)}) copy-start(f32[64,512]{1,0:T(8,128)} %param.14) | copy-start | bytes 393220
  31.1 17.5 %all-to-all-start = ((f32[8,1,8192]{2,1,0:T(1,128)}), f32[8,1,8192]{2,1,0:T(1,128)S(1)}, u32[]{:S(2)}, u32[]{:S(2)}) async-start(f32[8,1,8192]{2,1,0:T(1,128)} %stack.21), calls=%async_computation | async-start | bytes 524288 | tf_op jit(solution)/shard_map/all_to_all | solution.py:16
  57.9 4.8 collective-permute-start.4
  60.6 7.8 %collective-permute-start.7 = (f32[128,3,128]{2,1,0:T(4,128)S(1)}, f32[128,3,128]{2,1,0:T(4,128)S(1)}, u32[]{:S(2)}, u32[]{:S(2)}) collective-permute-start(f32[128,3,128]{2,1,0:T(4,128)S(1)} %get-tuple-element.35), channel_id=1, source_target_pairs={{0,1},{1,0},{2,3},{3,2},{4,5},{5,4},{6,7},{7,6},{8,9},{9,8},{10,11... | collective-permute-start | bytes 589832 | tf_op jit(solution)/shard_map/ppermute | solution.py:23
  60.9 9.0 %collective-permute-start.6 = (f32[128,3,128]{2,1,0:T(4,128)S(1)}, f32[128,3,128]{2,1,0:T(4,128)S(1)}, u32[]{:S(2)}, u32[]{:S(2)}) collective-permute-start(f32[128,3,128]{2,1,0:T(4,128)S(1)} %get-tuple-element.36), channel_id=1, source_target_pairs={{0,32},{8,40},{16,48},{24,56},{32,0},{40,8},{48,16},{56,24},{64,96... | collective-permute-start | bytes 589832 | tf_op jit(solution)/shard_map/ppermute | solution.py:23
  62.5 11.4 %collective-permute-start.5 = (f32[128,3,128]{2,1,0:T(4,128)S(1)}, f32[128,3,128]{2,1,0:T(4,128)S(1)}, u32[]{:S(2)}, u32[]{:S(2)}) collective-permute-start(f32[128,3,128]{2,1,0:T(4,128)S(1)} %get-tuple-element.37), channel_id=1, source_target_pairs={{0,16},{8,24},{16,0},{24,8},{32,48},{40,56},{48,32},{56,40},{64,80... | collective-permute-start | bytes 589832 | tf_op jit(solution)/shard_map/ppermute | solution.py:23
  104.3 6.2 %collective-permute-start.8 = (f32[128,3,128]{2,1,0:T(4,128)S(1)}, f32[128,3,128]{2,1,0:T(4,128)S(1)}, u32[]{:S(2)}, u32[]{:S(2)}) collective-permute-start(f32[128,3,128]{2,1,0:T(4,128)S(1)} %get-tuple-element.30), channel_id=1, source_target_pairs={{0,8},{8,0},{16,24},{24,16},{32,40},{40,32},{48,56},{56,48},{64,72... | collective-permute-start | bytes 589832 | tf_op jit(solution)/shard_map/ppermute | solution.py:23
  106.9 7.8 %collective-permute-start.11 = (f32[128,3,128]{2,1,0:T(4,128)S(1)}, f32[128,3,128]{2,1,0:T(4,128)S(1)}, u32[]{:S(2)}, u32[]{:S(2)}) collective-permute-start(f32[128,3,128]{2,1,0:T(4,128)S(1)} %get-tuple-element.31), channel_id=1, source_target_pairs={{0,1},{1,0},{2,3},{3,2},{4,5},{5,4},{6,7},{7,6},{8,9},{9,8},{10,11... | collective-permute-start | bytes 589832 | tf_op jit(solution)/shard_map/ppermute | solution.py:23
  107.2 9.6 %collective-permute-start.10 = (f32[128,3,128]{2,1,0:T(4,128)S(1)}, f32[128,3,128]{2,1,0:T(4,128)S(1)}, u32[]{:S(2)}, u32[]{:S(2)}) collective-permute-start(f32[128,3,128]{2,1,0:T(4,128)S(1)} %get-tuple-element.32), channel_id=1, source_target_pairs={{0,32},{8,40},{16,48},{24,56},{32,0},{40,8},{48,16},{56,24},{64,96... | collective-permute-start | bytes 589832 | tf_op jit(solution)/shard_map/ppermute | solution.py:23
  110.5 10.9 %collective-permute-start.9 = (f32[128,3,128]{2,1,0:T(4,128)S(1)}, f32[128,3,128]{2,1,0:T(4,128)S(1)}, u32[]{:S(2)}, u32[]{:S(2)}) collective-permute-start(f32[128,3,128]{2,1,0:T(4,128)S(1)} %get-tuple-element.33), channel_id=1, source_target_pairs={{0,16},{8,24},{16,0},{24,8},{32,48},{40,56},{48,32},{56,40},{64,80... | collective-permute-start | bytes 589832 | tf_op jit(solution)/shard_map/ppermute | solution.py:23
  240.4 5.0 collective-permute-start.12
  241.2 8.4 %collective-permute-start.15 = (f32[128,3,128]{2,1,0:T(4,128)S(1)}, f32[128,3,128]{2,1,0:T(4,128)S(1)}, u32[]{:S(2)}, u32[]{:S(2)}) collective-permute-start(f32[128,3,128]{2,1,0:T(4,128)S(1)} %get-tuple-element.27), channel_id=1, source_target_pairs={{0,1},{1,0},{2,3},{3,2},{4,5},{5,4},{6,7},{7,6},{8,9},{9,8},{10,11... | collective-permute-start | bytes 589832 | tf_op jit(solution)/shard_map/ppermute | solution.py:23
  242.9 9.0 %collective-permute-start.14 = (f32[128,3,128]{2,1,0:T(4,128)S(1)}, f32[128,3,128]{2,1,0:T(4,128)S(1)}, u32[]{:S(2)}, u32[]{:S(2)}) collective-permute-start(f32[128,3,128]{2,1,0:T(4,128)S(1)} %get-tuple-element.28), channel_id=1, source_target_pairs={{0,32},{8,40},{16,48},{24,56},{32,0},{40,8},{48,16},{56,24},{64,96... | collective-permute-start | bytes 589832 | tf_op jit(solution)/shard_map/ppermute | solution.py:23
  244.1 13.0 %collective-permute-start.13 = (f32[128,3,128]{2,1,0:T(4,128)S(1)}, f32[128,3,128]{2,1,0:T(4,128)S(1)}, u32[]{:S(2)}, u32[]{:S(2)}) collective-permute-start(f32[128,3,128]{2,1,0:T(4,128)S(1)} %get-tuple-element.29), channel_id=1, source_target_pairs={{0,16},{8,24},{16,0},{24,8},{32,48},{40,56},{48,32},{56,40},{64,80... | collective-permute-start | bytes 589832 | tf_op jit(solution)/shard_map/ppermute | solution.py:23
  289.4 5.0 collective-permute-start.16
  292.1 7.8 %collective-permute-start.19 = (f32[128,3,128]{2,1,0:T(4,128)S(1)}, f32[128,3,128]{2,1,0:T(4,128)S(1)}, u32[]{:S(2)}, u32[]{:S(2)}) collective-permute-start(f32[128,3,128]{2,1,0:T(4,128)S(1)} %get-tuple-element.23), channel_id=1, source_target_pairs={{0,1},{1,0},{2,3},{3,2},{4,5},{5,4},{6,7},{7,6},{8,9},{9,8},{10,11... | collective-permute-start | bytes 589832 | tf_op jit(solution)/shard_map/ppermute | solution.py:23
  292.4 9.2 %collective-permute-start.18 = (f32[128,3,128]{2,1,0:T(4,128)S(1)}, f32[128,3,128]{2,1,0:T(4,128)S(1)}, u32[]{:S(2)}, u32[]{:S(2)}) collective-permute-start(f32[128,3,128]{2,1,0:T(4,128)S(1)} %get-tuple-element.24), channel_id=1, source_target_pairs={{0,32},{8,40},{16,48},{24,56},{32,0},{40,8},{48,16},{56,24},{64,96... | collective-permute-start | bytes 589832 | tf_op jit(solution)/shard_map/ppermute | solution.py:23
  294.3 11.6 %collective-permute-start.17 = (f32[128,3,128]{2,1,0:T(4,128)S(1)}, f32[128,3,128]{2,1,0:T(4,128)S(1)}, u32[]{:S(2)}, u32[]{:S(2)}) collective-permute-start(f32[128,3,128]{2,1,0:T(4,128)S(1)} %get-tuple-element.25), channel_id=1, source_target_pairs={{0,16},{8,24},{16,0},{24,8},{32,48},{40,56},{48,32},{56,40},{64,80... | collective-permute-start | bytes 589832 | tf_op jit(solution)/shard_map/ppermute | solution.py:23
  416.3 3.7 collective-permute-start.20
  417.3 8.3 %collective-permute-start.23 = (f32[128,3,128]{2,1,0:T(4,128)S(1)}, f32[128,3,128]{2,1,0:T(4,128)S(1)}, u32[]{:S(2)}, u32[]{:S(2)}) collective-permute-start(f32[128,3,128]{2,1,0:T(4,128)S(1)} %get-tuple-element.19), channel_id=1, source_target_pairs={{0,1},{1,0},{2,3},{3,2},{4,5},{5,4},{6,7},{7,6},{8,9},{9,8},{10,11... | collective-permute-start | bytes 589832 | tf_op jit(solution)/shard_map/ppermute | solution.py:23
  419.0 9.0 %collective-permute-start.22 = (f32[128,3,128]{2,1,0:T(4,128)S(1)}, f32[128,3,128]{2,1,0:T(4,128)S(1)}, u32[]{:S(2)}, u32[]{:S(2)}) collective-permute-start(f32[128,3,128]{2,1,0:T(4,128)S(1)} %get-tuple-element.20), channel_id=1, source_target_pairs={{0,32},{8,40},{16,48},{24,56},{32,0},{40,8},{48,16},{56,24},{64,96... | collective-permute-start | bytes 589832 | tf_op jit(solution)/shard_map/ppermute | solution.py:23
  419.9 11.7 %collective-permute-start.21 = (f32[128,3,128]{2,1,0:T(4,128)S(1)}, f32[128,3,128]{2,1,0:T(4,128)S(1)}, u32[]{:S(2)}, u32[]{:S(2)}) collective-permute-start(f32[128,3,128]{2,1,0:T(4,128)S(1)} %get-tuple-element.21), channel_id=1, source_target_pairs={{0,16},{8,24},{16,0},{24,8},{32,48},{40,56},{48,32},{56,40},{64,80... | collective-permute-start | bytes 589832 | tf_op jit(solution)/shard_map/ppermute | solution.py:23
  456.3 0.9 copy-start.1
  466.1 5.8 collective-permute-start.24
  468.8 7.8 %collective-permute-start.27 = (f32[128,3,128]{2,1,0:T(4,128)S(1)}, f32[128,3,128]{2,1,0:T(4,128)S(1)}, u32[]{:S(2)}, u32[]{:S(2)}) collective-permute-start(f32[128,3,128]{2,1,0:T(4,128)S(1)} %get-tuple-element.15), channel_id=1, source_target_pairs={{0,1},{1,0},{2,3},{3,2},{4,5},{5,4},{6,7},{7,6},{8,9},{9,8},{10,11... | collective-permute-start | bytes 589832 | tf_op jit(solution)/shard_map/ppermute | solution.py:23
  469.1 9.0 %collective-permute-start.26 = (f32[128,3,128]{2,1,0:T(4,128)S(1)}, f32[128,3,128]{2,1,0:T(4,128)S(1)}, u32[]{:S(2)}, u32[]{:S(2)}) collective-permute-start(f32[128,3,128]{2,1,0:T(4,128)S(1)} %get-tuple-element.16), channel_id=1, source_target_pairs={{0,32},{8,40},{16,48},{24,56},{32,0},{40,8},{48,16},{56,24},{64,96... | collective-permute-start | bytes 589832 | tf_op jit(solution)/shard_map/ppermute | solution.py:23
  470.8 12.7 %collective-permute-start.25 = (f32[128,3,128]{2,1,0:T(4,128)S(1)}, f32[128,3,128]{2,1,0:T(4,128)S(1)}, u32[]{:S(2)}, u32[]{:S(2)}) collective-permute-start(f32[128,3,128]{2,1,0:T(4,128)S(1)} %get-tuple-element.17), channel_id=1, source_target_pairs={{0,16},{8,24},{16,0},{24,8},{32,48},{40,56},{48,32},{56,40},{64,80... | collective-permute-start | bytes 589832 | tf_op jit(solution)/shard_map/ppermute | solution.py:23
  492.1 90.8 %copy-start.2 = (f32[128,1536]{1,0:T(8,128)S(1)}, f32[128,1536]{1,0:T(8,128)}, u32[]{:S(2)}) copy-start(f32[128,1536]{1,0:T(8,128)} %copy-done.1) | copy-start | bytes 2359300
